TPU v7x, 32 devices: a whole 2x2x4 slice. The times are simulated.
32 devices in a mesh: parts: 2 (over y), seq: 4 (over z), tp: 4 (over x, core).
Axes of the slice: x: 2, y: 2, z: 4, core: 2. Of those that a mesh axis runs over, the one named last changes fastest.
Arguments:
- x_gate: bfloat16 [1024, 4096], P(('parts', 'seq'), 'tp'), parts along dimension 0, may hold values from -6 to 6
- x_key: bfloat16 [1024, 4096], P(('parts', 'seq'), 'tp'), parts along dimension 0, may hold values from -6 to 6
- x_value: bfloat16 [1024, 4096], P(('parts', 'seq'), 'tp'), parts along dimension 0, may hold values from -6 to 6
- conv_state: bfloat16 [254, 4096], P('parts', 'tp'), parts along dimension 0, may hold values from -6 to 6
- filter_taps: float32 [256, 128], P('tp'), may hold values from -0.875 to 0.875
- decay_rates: float32 [256], P('tp'), may hold values from 0.0005 to 0.1
- skip_gain: float32 [4096], P('tp'), may hold values from -1 to 1
- queries: bfloat16 [1024, 2048], P(('parts', 'seq'), 'tp'), parts along dimension 0, may hold values from -10 to 10
- stretch_keys: bfloat16 [1024, 2048], P(('parts', 'seq'), 'tp'), parts along dimension 0, may hold values from -10 to 10
- stretch_values: bfloat16 [1024, 2048], P(('parts', 'seq'), 'tp'), parts along dimension 0, may hold values from -6 to 6
- cache_keys: bfloat16 [64, 2048], P(('parts', 'seq'), 'tp'), parts along dimension 0, may hold values from -10 to 10
- cache_values: bfloat16 [64, 2048], P(('parts', 'seq'), 'tp'), parts along dimension 0, may hold values from -6 to 6
- prefix_len: int32 [2], P('parts'), parts along dimension 0, may hold values from 16 to 32
Outputs:
- hyena_out: bfloat16 [1024, 4096], P(('parts', 'seq'), 'tp'), parts along dimension 0
- attention_out: bfloat16 [1024, 2048], P(('parts', 'seq'), 'tp'), parts along dimension 0
There are 2 independent parts, one for each index of `parts`. A program takes and returns all parts, laid end to end along the dimension named above; an argument that names none is the same for every part. Nothing has to cross between parts.
Inputs may be any that keep to these rules, and one draw needn't show every extreme that they name: `prefix_len`: the number of leading cached positions that hold keys and values.
All inputs are finite; a program needn't handle non-finite values.
Results may differ from a plain program's by a relative error of at most 0.0056.
Values may be sent and summed in bfloat16 or wider, within the bound.
A program may use at most 128 MiB of HBM per device.

v0:
```python
import math

import jax
import jax.numpy as jnp
from jax import lax
from jax.sharding import PartitionSpec as P

HD = 128


far_position = 1 << 30


def shifted(value, axis, steps):
    count = lax.axis_size(axis)
    first, last = (max(0, -steps), min(count, count - steps))
    return lax.ppermute(value, axis, [(source, source + steps) for source in range(first, last)])


def on_device(
    x_gate,
    x_key,
    x_value,
    conv_state,
    filter_taps,
    decay_rates,
    skip_gain,
    queries,
    stretch_keys,
    stretch_values,
    cache_keys,
    cache_values,
    prefix_len,
):
    rows_dev = x_gate.shape[0]
    chans_dev = x_gate.shape[1]
    seq_index = lax.axis_index("seq")
    product_in = (x_key.astype(jnp.float32) * x_value.astype(jnp.float32)).astype(jnp.bfloat16)
    filter_reach = filter_taps.shape[1] - 1
    received = []
    taken = min(rows_dev, filter_reach)
    received.insert(0, shifted(product_in[rows_dev - taken :], "seq", 1))
    earlier = received[0]
    padded_state = jnp.concatenate(
        [conv_state, jnp.zeros((filter_reach, chans_dev), jnp.bfloat16)], axis=0
    )
    earlier = earlier + lax.dynamic_slice_in_dim(
        padded_state, seq_index * rows_dev, filter_reach, 0
    )
    extended = jnp.concatenate([earlier, product_in], axis=0)
    span_total = rows_dev + filter_reach
    tap_ramp = lax.iota(jnp.float32, filter_reach + 1)
    filters = (filter_taps * jnp.exp(-decay_rates[:, None] * tap_ramp[None, :])).astype(
        jnp.bfloat16
    )
    group_count = filters.shape[0]
    group_width = chans_dev // group_count
    skew_period = span_total + rows_dev - 1
    reversed_taps = jnp.concatenate(
        [filters[:, ::-1], jnp.zeros((group_count, skew_period - filter_reach - 1), jnp.bfloat16)],
        axis=1,
    )
    group_block = min(group_count, 16)
    conv_parts = []
    for first_group in range(0, group_count, group_block):
        taps_block = reversed_taps[first_group : first_group + group_block]
        toeplitz = jnp.tile(taps_block, (1, rows_dev + 1))[:, : rows_dev * (skew_period - 1)]
        toeplitz = toeplitz.reshape(group_block, rows_dev, skew_period - 1)[:, :, :span_total]
        columns = extended[:, first_group * group_width : (first_group + group_block) * group_width]
        columns = columns.reshape(span_total, group_block, group_width)
        conv_block = jnp.einsum(
            "gts,sgc->tgc", toeplitz, columns, preferred_element_type=jnp.float32
        )
        conv_parts.append(conv_block.reshape(rows_dev, group_block * group_width))
    filtered = jnp.concatenate(conv_parts, axis=1)
    hyena_out = (
        x_gate.astype(jnp.float32)
        * (filtered + skip_gain[None, :] * product_in.astype(jnp.float32))
    ).astype(jnp.bfloat16)
    head_count = queries.shape[1] // HD
    half_rows = rows_dev // 2
    scale_factor = 1.0 / math.sqrt(HD)
    half_ramp = lax.iota(jnp.int32, half_rows)
    second_base = seq_index * rows_dev + half_rows
    query_pos = jnp.stack([seq_index * rows_dev + half_ramp, second_base + half_ramp])
    query_heads = queries.reshape(2, half_rows, head_count, HD)
    limit_len = prefix_len[0]

    def consume(state, key_rows, value_rows, key_pos):
        row_total = key_rows.shape[0]
        if row_total <= 512:
            block_rows = row_total
            block_count = 1
        else:
            block_rows = 512
            block_count = -(-row_total // 512)
        key_blocks = key_rows.reshape(block_count, block_rows, head_count, HD)
        value_blocks = value_rows.reshape(block_count, block_rows, head_count, HD)
        pos_blocks = key_pos.reshape(block_count, block_rows)

        def one_block(block_step, inner):
            maxima, totals, sums = inner
            key_block = lax.dynamic_index_in_dim(key_blocks, block_step, 0, keepdims=False)
            value_block = lax.dynamic_index_in_dim(value_blocks, block_step, 0, keepdims=False)
            pos_block = lax.dynamic_index_in_dim(pos_blocks, block_step, 0, keepdims=False)
            for half_index in range(2):
                half_queries = query_heads[half_index]
                half_pos = query_pos[half_index]

                def update(parts):
                    run_max, run_total, run_sum = parts
                    scores = (
                        jnp.einsum(
                            "thd,shd->hts",
                            half_queries,
                            key_block,
                            preferred_element_type=jnp.float32,
                        )
                        * scale_factor
                    )
                    allowed = (pos_block[None, :] <= half_pos[:, None])[None]
                    scores = jnp.where(allowed, scores, -1e30)
                    new_max = jnp.maximum(run_max, jnp.max(scores, axis=2))
                    weights = jnp.where(allowed, jnp.exp(scores - new_max[:, :, None]), 0.0)
                    factor = jnp.exp(run_max - new_max)
                    new_total = run_total * factor + jnp.sum(weights, axis=2)
                    new_sum = run_sum * factor[:, :, None] + jnp.einsum(
                        "hts,shd->htd",
                        weights.astype(jnp.bfloat16),
                        value_block,
                        preferred_element_type=jnp.float32,
                    )
                    return (new_max, new_total, new_sum)

                def unchanged(parts):
                    return parts

                result = lax.cond(
                    jnp.min(pos_block) <= jnp.max(half_pos),
                    update,
                    unchanged,
                    (maxima[half_index], totals[half_index], sums[half_index]),
                )
                maxima = maxima.at[half_index].set(result[0])
                totals = totals.at[half_index].set(result[1])
                sums = sums.at[half_index].set(result[2])
            return (maxima, totals, sums)

        return lax.fori_loop(0, block_count, one_block, state)

    initial = (
        jnp.full((2, head_count, half_rows), -1e30, jnp.float32),
        jnp.zeros((2, head_count, half_rows), jnp.float32),
        jnp.zeros((2, head_count, half_rows, HD), jnp.float32),
    )
    cache_whole = (
        lax.all_gather(cache_keys, "seq", axis=0, tiled=True),
        lax.all_gather(cache_values, "seq", axis=0, tiled=True),
    )
    cache_ids = lax.iota(jnp.int32, cache_whole[0].shape[0])
    cache_pos = jnp.where(cache_ids < limit_len, -1, far_position)
    start_state = consume(initial, cache_whole[0], cache_whole[1], cache_pos)
    piece = (
        lax.all_gather(stretch_keys, "seq", axis=0, tiled=True),
        lax.all_gather(stretch_values, "seq", axis=0, tiled=True),
    )
    key_pos = lax.iota(jnp.int32, piece[0].shape[0])
    state = consume(start_state, piece[0], piece[1], key_pos)
    normalized = state[2] / state[1][:, :, :, None]
    result_rows = (
        normalized.transpose(0, 2, 1, 3).reshape(rows_dev, head_count * HD).astype(jnp.bfloat16)
    )
    return (hyena_out, result_rows)


def solution(mesh):
    placed = (
        P(("parts", "seq"), "tp"),
        P(("parts", "seq"), "tp"),
        P(("parts", "seq"), "tp"),
        P("parts", "tp"),
        P("tp", None),
        P("tp"),
        P("tp"),
        P(("parts", "seq"), "tp"),
        P(("parts", "seq"), "tp"),
        P(("parts", "seq"), "tp"),
        P(("parts", "seq"), "tp"),
        P(("parts", "seq"), "tp"),
        P("parts"),
    )
    return jax.shard_map(
        on_device,
        mesh=mesh,
        in_specs=placed,
        out_specs=(P(("parts", "seq"), "tp"), P(("parts", "seq"), "tp")),
        check_vma=False,
    )
```

profile of v0, /device:TPU:0, one launch (start us, length us, event | category | flops | bytes accessed | tf_op | source)
XLA Modules:
  0.0 127.4 jit_solution(4712536788235111334)
XLA Ops:
  0.7 1.1 multiply_convert_fusion
  2.5 5.8 %collective-permute-start = (bf16[127,1024]{1,0:T(8,128)(2,1)}, bf16[127,1024]{1,0:T(8,128)(2,1)}, u32[]{:S(2)}, u32[]{:S(2)}) collective-permute-start(bf16[127,1024]{1,0:T(8,128)(2,1)} %slice.481), channel_id=1, source_target_pairs={{0,4},{4,8},{8,12},{1,5},{5,9},{9,13},{2,6},{6,10},{10,14},{3,7},{... | collective-permute-start | bytes 780296 | tf_op jit(solution)/shard_map/ppermute | solution.py:17
  15.1 13.1 %all_gather.12 = bf16[32,512]{1,0:T(8,128)(2,1)S(1)} all-gather(bf16[8,512]{1,0:T(8,128)(2,1)S(1)} %copy-done.13), channel_id=1, replica_groups=mesh['parts'=2,'seq'=4,'tp'=4] {'seq'}, dimensions={0}, use_global_device_ids=true | all-gather | bytes 40960 | tf_op jit(solution)/shard_map/all_gather | solution.py:157
  28.3 13.1 %all_gather.13 = bf16[32,512]{1,0:T(8,128)(2,1)S(1)} all-gather(bf16[8,512]{1,0:T(8,128)(2,1)S(1)} %copy-done.14), channel_id=1, replica_groups=mesh['parts'=2,'seq'=4,'tp'=4] {'seq'}, dimensions={0}, use_global_device_ids=true | all-gather | bytes 40960 | tf_op jit(solution)/shard_map/all_gather | solution.py:158
  41.5 8.2 %conditional.4 = (f32[4,64]{1,0:T(4,128)}, f32[4,64]{1,0:T(4,128)}, f32[4,64,128]{2,1,0:T(8,128)}, f32[1,4,64,128]{3,2,1,0:T(8,128)S(1)}, (f32[4,64]{1,0:T(4,128...) conditional(s32[]{:T(128)} %convert_element_type.67, ...), branch_computations={%region_2.3_spmd, %region_3.0_spmd} | conditional | flops 4336128 | bytes 1044936 | solution.py:138
  43.1 1.3 multiply_add_fusion
  44.4 1.6 %convolution_add_fusion = f32[4,64,128]{2,1,0:T(8,128)} fusion(f32[4,64,128]{2,1,0:T(8,128)S(1)} %get-tuple-element.460, f32[4,64]{1,0:T(4,128)S(1)} %get-tuple-element.562, f32[4,64,32]{1,2,0:T(8,128)S(1)} %get-tuple-element.570, bf16[32,4,128]{2,1,0:T(4,128)(2,1)S(1)} %get-tuple-element.536, f32[4,64]{1,0:T(4,128)} %max.10, ...), kind=kOutput, calls=%fused_computation | convolution fusion | flops 2187264 | bytes 331776 | tf_op jit(solution)/shard_map/while/body/eval_jaxpr/cond/branch_1_fun/hts,shd->htd/dot_general | solution.py:127
  49.8 14.5 %all_gather.14 = bf16[512,512]{0,1:T(8,128)(2,1)S(1)} all-gather(bf16[128,512]{0,1:T(8,128)(2,1)S(1)} %copy.38), channel_id=1, replica_groups=mesh['parts'=2,'seq'=4,'tp'=4] {'seq'}, dimensions={0}, use_global_device_ids=true | all-gather | bytes 655360 | tf_op jit(solution)/shard_map/all_gather | solution.py:164
  64.5 13.8 %all_gather.15 = bf16[512,512]{0,1:T(8,128)(2,1)S(1)} all-gather(bf16[128,512]{0,1:T(8,128)(2,1)S(1)} %copy.39), channel_id=1, replica_groups=mesh['parts'=2,'seq'=4,'tp'=4] {'seq'}, dimensions={0}, use_global_device_ids=true | all-gather | bytes 655360 | tf_op jit(solution)/shard_map/all_gather | solution.py:165
  78.3 3.1 %conditional.5 = (f32[1,4,64,128]{3,2,1,0:T(8,128)S(1)}, f32[1,4,64]{2,1,0:T(4,128)S(1)}, f32[1,4,64]{2,1,0:T(4,128)}) conditional(s32[]{:T(128)} %convert_element_type.68, (f32[4,64]{1,0:T(4,128)S(1)}, f32[4,64]{1,0:T(4,128)S(1)}, f32[4,64,128]{2,1,0:T(8,128)S(1)}) %tuple.188, (s32[32]{0:T(128)S(1)}, s32[64]{0:T(128)S(1)}, ...), branch_computations={%region_7.8_spmd, %region_8.11_spmd} | conditional | flops 4336128 | bytes 514456 | solution.py:138
  81.5 3.3 %conditional.6 = (f32[1,4,64,128]{3,2,1,0:T(8,128)S(1)}, f32[1,4,64]{2,1,0:T(4,128)S(1)}) conditional(s32[]{:T(128)} %convert_element_type.69, (f32[4,64]{1,0:T(4,128)S(1)}, f32[4,64,128]{2,1,0:T(8,128)S(1)}) %get-tuple-element.512, (s32[512]{0:T(512)S(1)}, s32[64]{0:T(128)S(1)}, bf16[64,4,128]{2,1,0:T(4,128)(2,1)S(1)}, ...), branch_computations={%region_11.12_spmd, %region_12.15_spmd} | conditional | flops 68387328 | bytes 3096848 | solution.py:138
  83.5 1.2 fusion.24
  85.8 1.2 conditional.7
  87.9 1.2 tile.43
  89.2 4.4 %reshape.774 = bf16[16,128,381]{2,1,0:T(8,128)(2,1)} reshape(bf16[16,48768]{1,0:T(8,128)(2,1)S(1)} %slice.494) | data formatting | bytes 3121152 | tf_op jit(solution)/shard_map/reshape | solution.py:68
  93.8 1.2 tile.41
  95.1 4.4 %reshape.771 = bf16[16,128,381]{2,1,0:T(8,128)(2,1)} reshape(bf16[16,48768]{1,0:T(8,128)(2,1)S(1)} %slice.492) | data formatting | bytes 3121152 | tf_op jit(solution)/shard_map/reshape | solution.py:68
  99.7 1.2 tile.19
  101.0 4.4 %reshape.768 = bf16[16,128,381]{2,1,0:T(8,128)(2,1)} reshape(bf16[16,48768]{1,0:T(8,128)(2,1)S(1)} %slice.488) | data formatting | bytes 3121152 | tf_op jit(solution)/shard_map/reshape | solution.py:68
  105.5 1.2 tile.17
  106.9 4.4 %reshape.765 = bf16[16,128,381]{2,1,0:T(8,128)(2,1)} reshape(bf16[16,48768]{1,0:T(8,128)(2,1)S(1)} %slice.484) | data formatting | bytes 3121152 | tf_op jit(solution)/shard_map/reshape | solution.py:68
  112.2 1.1 fusion.54
  114.2 1.0 copy.27
  115.2 1.0 fusion.44
  116.2 1.8 %copy.31 = f32[128,256]{1,0:T(8,128)} copy(f32[128,256]{0,1:T(8,128)} %bitcast.80) | data formatting | bytes 262144 | tf_op jit(solution)/shard_map/reshape | solution.py:74
  118.0 1.0 copy.26
  119.0 1.0 fusion.46
  120.1 1.8 %copy.30 = f32[128,256]{1,0:T(8,128)} copy(f32[128,256]{0,1:T(8,128)} %bitcast.82) | data formatting | bytes 262144 | tf_op jit(solution)/shard_map/reshape | solution.py:74
  121.8 1.0 copy.25
  122.9 1.0 fusion.48
  123.9 1.1 copy.29
  125.0 1.0 copy.24
  (107 shorter events, 20.6 us)
Async XLA Ops:
  0.6 14.5 %copy-start.13 = (bf16[8,512]{1,0:T(8,128)(2,1)S(1)}, bf16[8,512]{1,0:T(8,128)(2,1)}, u32[]{:S(2)}) copy-start(bf16[8,512]{1,0:T(8,128)(2,1)} %param.55) | copy-start | bytes 24580
  0.6 27.6 %copy-start.14 = (bf16[8,512]{1,0:T(8,128)(2,1)S(1)}, bf16[8,512]{1,0:T(8,128)(2,1)}, u32[]{:S(2)}) copy-start(bf16[8,512]{1,0:T(8,128)(2,1)} %param.56) | copy-start | bytes 24580
  2.5 47.2 %copy-start.10 = (bf16[128,512]{1,0:T(8,128)(2,1)S(1)}, bf16[128,512]{1,0:T(8,128)(2,1)}, u32[]{:S(2)}) copy-start(bf16[128,512]{1,0:T(8,128)(2,1)} %param.53) | copy-start | bytes 393220
  2.5 109.7 %collective-permute-start = (bf16[127,1024]{1,0:T(8,128)(2,1)}, bf16[127,1024]{1,0:T(8,128)(2,1)}, u32[]{:S(2)}, u32[]{:S(2)}) collective-permute-start(bf16[127,1024]{1,0:T(8,128)(2,1)} %slice.481), channel_id=1, source_target_pairs={{0,4},{4,8},{8,12},{1,5},{5,9},{9,13},{2,6},{6,10},{10,14},{3,7},{... | collective-permute-start | bytes 780296 | tf_op jit(solution)/shard_map/ppermute | solution.py:17
  41.5 22.9 %copy-start.11 = (bf16[128,512]{1,0:T(8,128)(2,1)S(1)}, bf16[128,512]{1,0:T(8,128)(2,1)}, u32[]{:S(2)}) copy-start(bf16[128,512]{1,0:T(8,128)(2,1)} %param.54) | copy-start | bytes 393220
  81.5 3.4 %copy-start.16 = (f32[64]{0:T(128)S(1)}, f32[64]{0:T(128)}, u32[]{:S(2)}) copy-start(f32[64]{0:T(128)} %param.50) | copy-start | bytes 772
  81.5 3.4 %copy-start.12 = (f32[64,128]{1,0:T(8,128)S(1)}, f32[64,128]{1,0:T(8,128)}, u32[]{:S(2)}) copy-start(f32[64,128]{1,0:T(8,128)} %param.49) | copy-start | bytes 98308
  87.0 0.7 copy-start.4
  106.9 4.4 %copy-start.5 = (f32[2,4,64,128]{3,2,1,0:T(8,128)S(1)}, f32[2,4,64,128]{3,2,1,0:T(8,128)}, u32[]{:S(2)}) copy-start(f32[2,4,64,128]{3,2,1,0:T(8,128)} %copy-done.4) | copy-start | bytes 786436
  106.9 5.3 %copy-start.9 = (bf16[127,1024]{1,0:T(8,128)(2,1)S(1)}, bf16[127,1024]{1,0:T(8,128)(2,1)}, u32[]{:S(2)}) copy-start(bf16[127,1024]{1,0:T(8,128)(2,1)} %param.48) | copy-start | bytes 780292
  111.3 3.9 %copy-start = (bf16[16,128,381]{2,1,0:T(8,128)(2,1)S(1)}, bf16[16,128,381]{2,1,0:T(8,128)(2,1)}, u32[]{:S(2)}) copy-start(bf16[16,128,381]{2,1,0:T(8,128)(2,1)} %reshape.774) | copy-start | bytes 4681732
  113.3 5.7 %copy-start.1 = (bf16[16,128,381]{2,1,0:T(8,128)(2,1)S(1)}, bf16[16,128,381]{2,1,0:T(8,128)(2,1)}, u32[]{:S(2)}) copy-start(bf16[16,128,381]{2,1,0:T(8,128)(2,1)} %reshape.771) | copy-start | bytes 4681732
  116.2 6.6 %copy-start.2 = (bf16[16,128,381]{2,1,0:T(8,128)(2,1)S(1)}, bf16[16,128,381]{2,1,0:T(8,128)(2,1)}, u32[]{:S(2)}) copy-start(bf16[16,128,381]{2,1,0:T(8,128)(2,1)} %reshape.768) | copy-start | bytes 4681732
  120.1 5.9 %copy-start.3 = (bf16[16,128,381]{2,1,0:T(8,128)(2,1)S(1)}, bf16[16,128,381]{2,1,0:T(8,128)(2,1)}, u32[]{:S(2)}) copy-start(bf16[16,128,381]{2,1,0:T(8,128)(2,1)} %reshape.765) | copy-start | bytes 4681732
  122.9 3.6 %copy-start.15 = (f32[1024]{0:T(1024)S(1)}, f32[1024]{0:T(1024)}, u32[]{:S(2)}) copy-start(f32[1024]{0:T(1024)} %param.51) | copy-start | bytes 12292
  123.9 2.6 %copy-start.6 = (f32[128,256]{1,0:T(8,128)S(1)}, f32[128,256]{1,0:T(8,128)}, u32[]{:S(2)}) copy-start(f32[128,256]{1,0:T(8,128)} %copy.31) | copy-start | bytes 393220
  123.9 2.6 %copy-start.7 = (f32[128,256]{1,0:T(8,128)S(1)}, f32[128,256]{1,0:T(8,128)}, u32[]{:S(2)}) copy-start(f32[128,256]{1,0:T(8,128)} %copy.30) | copy-start | bytes 393220
  123.9 2.6 %copy-start.8 = (bf16[128,1024]{1,0:T(8,128)(2,1)S(1)}, bf16[128,1024]{1,0:T(8,128)(2,1)}, u32[]{:S(2)}) copy-start(bf16[128,1024]{1,0:T(8,128)(2,1)} %param.45) | copy-start | bytes 786436
where the time goes:
time: 128 us; the launch traced here: 127 us
  blocking collectives  54.6 us (43%)
  local copies, waits for them, and re-layouts  39.7 us (31%)
  other arithmetic  12.9 us (10%)
  matrix products  8.49 us (7%)
  starting transfers between devices  5.75 us (4%)
  between operations  5.67 us (4%)
    reshape x4, local copies, waits for them, and re-layouts, on_device(): toeplitz.reshape(group_block, rows_dev, skew_period - 1)[:, :, :span_total]  17.5 us
    all_gather x1, blocking collectives, on_device(): lax.all_gather(stretch_keys, 'seq', axis=0, tiled=True)  14.5 us
    all_gather x1, blocking collectives, on_device(): lax.all_gather(stretch_values, 'seq', axis=0, tiled=True)  13.8 us
    all_gather x1, blocking collectives, on_device(): lax.all_gather(cache_keys, 'seq', axis=0, tiled=True)  13.1 us
    all_gather x1, blocking collectives, on_device(): lax.all_gather(cache_values, 'seq', axis=0, tiled=True)  13.1 us
    ppermute x1, starting transfers between devices, shifted(): lax.ppermute(value, axis, [(source, source + steps) for source in range(f...  5.75 us
    another operation x8, local copies, waits for them, and re-layouts, on_device(): jnp.tile(taps_block, (1, rows_dev + 1))[:, :rows_dev * (skew_period - 1)]  5.58 us
    reshape x4, local copies, waits for them, and re-layouts, on_device(): conv_parts.append(conv_block.reshape(rows_dev, group_block * group_width))  4.73 us
  transfers between devices with their start and end apart: 1, of which 0 were waited for; matrix products, arithmetic and copies ran while one was open for 34% of the time, Pallas kernels for 0%

commit v1 on v0

--- a/solution.py
+++ b/solution.py
@@ -3,6 +3,8 @@
 import jax
 import jax.numpy as jnp
 from jax import lax
+from jax.experimental import pallas as pl
+from jax.experimental.pallas import tpu as pltpu
 from jax.sharding import PartitionSpec as P
 
 HD = 128
@@ -17,7 +19,7 @@
     return lax.ppermute(value, axis, [(source, source + steps) for source in range(first, last)])
 
 
-def on_device(
+def general_form(
     x_gate,
     x_key,
     x_value,
@@ -173,6 +175,447 @@
     return (hyena_out, result_rows)
 
 
+MESH = pl.DeviceIdType.MESH
+F32 = jnp.float32
+BF16 = jnp.bfloat16
+
+
+def remote(src, dst, send_sem, recv_sem, target):
+    return pltpu.make_async_remote_copy(
+        src_ref=src,
+        dst_ref=dst,
+        send_sem=send_sem,
+        recv_sem=recv_sem,
+        device_id={"seq": target},
+        device_id_type=MESH,
+    )
+
+
+def short_kernel(
+    x_gate, x_key, x_value, conv_state, filter_taps, decay_rates, skip_gain,
+    queries, stretch_keys, stretch_values, cache_keys, cache_values, prefix_len,
+    hyena_out, attention_out,
+    gate_v, key_v, value_v, state_v, taps_v, decay_v, skip_v, q_v, k_v, v_v,
+    cache_k, cache_v, k_in, v_in, q_in, product_v, earlier_v, shifted_v,
+    reversed_v, lower_v, upper_v, local_v, out_v,
+    own_acc, own_stat, part_out, stat_out, part_in, stat_in, att_v,
+    load_sem, send_sem, recv_sem, cache_send, cache_recv, out_sem,
+):
+    me = lax.axis_index("seq")
+    rows, chans = gate_v.shape
+    groups, taps = taps_v.shape
+    width = chans // groups
+    heads = q_v.shape[1] // HD
+    scale_factor = 1.0 / math.sqrt(HD)
+
+    loads = {}
+    for at, (name, src, dst) in enumerate(
+        [
+            ("key", x_key, key_v),
+            ("value", x_value, value_v),
+            ("taps", filter_taps, taps_v),
+            ("decay", decay_rates, decay_v),
+            ("q", queries, q_v),
+            ("k", stretch_keys, k_v),
+            ("v", stretch_values, v_v),
+            ("skip", skip_gain, skip_v),
+            ("gate", x_gate, gate_v),
+            ("state", conv_state, state_v),
+            ("ck", cache_keys, cache_k.at[me]),
+            ("cv", cache_values, cache_v.at[me]),
+        ]
+    ):
+        loads[name] = pltpu.make_async_copy(src, dst, load_sem.at[at])
+        loads[name].start()
+
+    barrier = pltpu.get_barrier_semaphore()
+    for step in range(1, 4):
+        pl.semaphore_signal(
+            barrier, inc=1, device_id={"seq": lax.rem(me + step, 4)}, device_id_type=MESH
+        )
+    pl.semaphore_wait(barrier, 3)
+
+    send_k = remote(stretch_keys, k_in, send_sem.at[0], recv_sem.at[0], 1)
+    send_v = remote(stretch_values, v_in, send_sem.at[1], recv_sem.at[1], 1)
+    send_q2 = remote(queries, q_in.at[0], send_sem.at[2], recv_sem.at[2], 1)
+    send_q3 = remote(queries, q_in.at[1], send_sem.at[3], recv_sem.at[3], 1)
+    send_q3_near = remote(queries, q_in.at[1], send_sem.at[2], recv_sem.at[3], 2)
+    send_product = remote(
+        product_v, earlier_v, send_sem.at[4], recv_sem.at[4], lax.rem(me + 1, 4)
+    )
+    send_part_near = remote(part_out.at[0], part_in.at[0], send_sem.at[5], recv_sem.at[5], 2)
+    send_stat_near = remote(stat_out.at[0], stat_in.at[0], send_sem.at[6], recv_sem.at[6], 2)
+    send_part_far = remote(part_out.at[1], part_in.at[0], send_sem.at[7], recv_sem.at[5], 3)
+    send_stat_far = remote(stat_out.at[1], stat_in.at[0], send_sem.at[8], recv_sem.at[6], 3)
+    send_part_last = remote(part_out.at[1], part_in.at[1], send_sem.at[5], recv_sem.at[7], 3)
+    send_stat_last = remote(stat_out.at[1], stat_in.at[1], send_sem.at[6], recv_sem.at[8], 3)
+
+    @pl.when(me == 0)
+    def _():
+        send_k.start()
+        send_v.start()
+
+    @pl.when(me == 2)
+    def _():
+        send_q2.start()
+
+    @pl.when(me == 3)
+    def _():
+        send_q3.start()
+        send_q3_near.start()
+
+    cache_copies = []
+    for step in range(1, 4):
+        target = lax.rem(me + step, 4)
+        for which, (src, dst) in enumerate(
+            [(cache_keys, cache_k), (cache_values, cache_v)]
+        ):
+            copy = remote(
+                src, dst.at[me], cache_send.at[which, step - 1], cache_recv.at[which, me], target
+            )
+            copy.start()
+            cache_copies.append(copy)
+
+    loads["key"].wait()
+    loads["value"].wait()
+    product_v[...] = (key_v[...].astype(F32) * value_v[...].astype(F32)).astype(BF16)
+
+    @pl.when(me < 3)
+    def _():
+        send_product.start()
+
+    loads["taps"].wait()
+    loads["decay"].wait()
+    row_id = lax.broadcasted_iota(jnp.int32, (groups, groups), 0)
+    col_id = lax.broadcasted_iota(jnp.int32, (groups, groups), 1)
+    rates = jnp.sum(
+        jnp.where(row_id == col_id, decay_v[...], 0.0), axis=1, keepdims=True
+    )
+    ramp = lax.broadcasted_iota(jnp.int32, (groups, taps), 1).astype(F32)
+    filters = (taps_v[...] * jnp.exp(-rates * ramp)).astype(BF16)
+    from_id = lax.broadcasted_iota(jnp.int32, (taps, taps), 0)
+    to_id = lax.broadcasted_iota(jnp.int32, (taps, taps), 1)
+    total_id = from_id + to_id
+    flip = jnp.where((total_id == 0) | (total_id == taps), 1.0, 0.0).astype(BF16)
+    reversed_v[...] = jnp.dot(filters, flip, preferred_element_type=F32)
+    below = to_id <= from_id
+
+    def build(pair, carry):
+        for half in range(2):
+            row = reversed_v[pl.ds(pair * 2 + half, 1), :]
+            circ = pltpu.roll(
+                jnp.broadcast_to(row, (rows, taps)), 0, 1, stride=1, stride_axis=0
+            )
+            lanes = pl.ds(half * taps, taps)
+            lower_v[pair, :, lanes] = jnp.where(below, circ, 0.0).astype(BF16)
+            upper_v[pair, :, lanes] = jnp.where(below, 0.0, circ).astype(BF16)
+        return carry
+
+    lax.fori_loop(0, groups // 2, build, 0)
+
+    lane = lax.broadcasted_iota(jnp.int32, (1, 128), 1)
+    odd_lane = lax.rem(lane // width, 2) == 1
+    odd = jnp.where(odd_lane, 1.0, 0.0).astype(BF16)
+    even = jnp.where(odd_lane, 0.0, 1.0).astype(BF16)
+    pair_of = lax.broadcasted_iota(jnp.int32, (rows, 128), 1) // (2 * width)
+    pairs = 128 // (2 * width)
+
+    def filtered(matrix_ref, block, tile):
+        stacked = jnp.concatenate([block * even, block * odd], axis=0)
+        total = None
+        for at in range(pairs):
+            term = jnp.dot(
+                matrix_ref[tile * pairs + at], stacked, preferred_element_type=F32
+            )
+            total = term if total is None else jnp.where(pair_of == at, term, total)
+        return total
+
+    loads["skip"].wait()
+    for tile in range(chans // 128):
+        cols = slice(tile * 128, (tile + 1) * 128)
+        block = product_v[:, cols]
+        local_v[:, cols] = filtered(lower_v, block, tile) + skip_v[:, cols] * block.astype(F32)
+
+    loads["q"].wait()
+    loads["k"].wait()
+    loads["v"].wait()
+    loads["ck"].wait()
+    loads["cv"].wait()
+    for step in range(1, 4):
+        source = lax.rem(me + step, 4)
+        for which, (src, dst) in enumerate(
+            [(cache_keys, cache_k), (cache_values, cache_v)]
+        ):
+            remote(
+                src, dst.at[source], cache_send.at[which, step - 1],
+                cache_recv.at[which, source], source,
+            ).wait_recv()
+
+    def joined(ref, cols):
+        return jnp.concatenate(
+            [ref[at, :, cols].astype(F32) for at in range(4)], axis=0
+        ).astype(BF16)
+
+    cache_rows = 4 * cache_k.shape[1]
+    causal = to_id >= from_id
+    in_prefix = (
+        lax.broadcasted_iota(jnp.int32, (cache_rows, rows), 0) < prefix_len[0]
+    )
+
+    def attend(query, blocks):
+        scores = []
+        for key, value, allowed in blocks:
+            score = (
+                lax.dot_general(
+                    key, query, (((1,), (1,)), ((), ())), preferred_element_type=F32
+                )
+                * scale_factor
+            )
+            if allowed is not None:
+                score = jnp.where(allowed, score, -1e30)
+            scores.append(score)
+        top = jnp.max(scores[0], axis=0, keepdims=True)
+        for score in scores[1:]:
+            top = jnp.maximum(top, jnp.max(score, axis=0, keepdims=True))
+        total, mixed = 0.0, 0.0
+        for score, (key, value, allowed) in zip(scores, blocks):
+            weight = jnp.exp(score - top)
+            if allowed is not None:
+                weight = jnp.where(allowed, weight, 0.0)
+            total = total + jnp.sum(weight, axis=0, keepdims=True)
+            mixed = mixed + lax.dot_general(
+                value, weight.astype(BF16), (((0,), (0,)), ((), ())),
+                preferred_element_type=F32,
+            )
+        return top, total, mixed
+
+    def head_cols(head):
+        return slice(head * HD, (head + 1) * HD)
+
+    def own_blocks(head):
+        cols = head_cols(head)
+        return [
+            (joined(cache_k, cols), joined(cache_v, cols), in_prefix),
+            (k_v[:, cols], v_v[:, cols], causal),
+        ]
+
+    def keep(head, result):
+        own_stat[head : head + 1, :] = result[0]
+        own_stat[heads + head : heads + head + 1, :] = result[1]
+        own_acc[head] = result[2]
+
+    def give(slot, head, result):
+        stat_out[slot, head : head + 1, :] = result[0]
+        stat_out[slot, heads + head : heads + head + 1, :] = result[1]
+        part_out[slot, head] = (result[2] / result[1]).astype(BF16)
+
+    @pl.when(me != 1)
+    def _():
+        for head in range(heads):
+            keep(head, attend(q_v[:, head_cols(head)], own_blocks(head)))
+
+    @pl.when(me == 1)
+    def _():
+        send_k.wait_recv()
+        send_v.wait_recv()
+
+        def shared_blocks(cols):
+            return [
+                (k_in[:, cols], v_in[:, cols], None),
+                (k_v[:, cols], v_v[:, cols], None),
+            ]
+
+        for slot, arrival, part, stat in (
+            (1, send_q3, send_part_far, send_stat_far),
+            (0, send_q2, send_part_near, send_stat_near),
+        ):
+            arrival.wait_recv()
+            for head in range(heads):
+                cols = head_cols(head)
+                give(slot, head, attend(q_in[slot, :, cols], shared_blocks(cols)))
+            part.start()
+            stat.start()
+        for head in range(heads):
+            cols = head_cols(head)
+            keep(
+                head,
+                attend(
+                    q_v[:, cols], own_blocks(head) + [(k_in[:, cols], v_in[:, cols], None)]
+                ),
+            )
+
+    @pl.when(me == 2)
+    def _():
+        send_q3_near.wait_recv()
+        for head in range(heads):
+            cols = head_cols(head)
+            give(1, head, attend(q_in[1, :, cols], [(k_v[:, cols], v_v[:, cols], None)]))
+        send_part_last.start()
+        send_stat_last.start()
+
+    loads["state"].wait()
+
+    @pl.when(me == 0)
+    def _():
+        shifted_v[0:1, :] = jnp.zeros((1, chans), F32)
+        shifted_v[pl.ds(1, rows - 1), :] = state_v[...].astype(F32)
+        earlier_v[...] = shifted_v[...].astype(BF16)
+
+    @pl.when(me > 0)
+    def _():
+        send_product.wait_recv()
+
+    loads["gate"].wait()
+    for tile in range(chans // 128):
+        cols = slice(tile * 128, (tile + 1) * 128)
+        whole = local_v[:, cols] + filtered(upper_v, earlier_v[:, cols], tile)
+        out_v[:, cols] = (gate_v[:, cols].astype(F32) * whole).astype(BF16)
+    hyena_write = pltpu.make_async_copy(out_v, hyena_out, out_sem.at[0])
+    hyena_write.start()
+
+    def finish(slots):
+        for head in range(heads):
+            top = own_stat[head : head + 1, :]
+            tops = [stat_in[slot, head : head + 1, :] for slot in slots]
+            best = top
+            for other in tops:
+                best = jnp.maximum(best, other)
+            share = jnp.exp(top - best)
+            total = own_stat[heads + head : heads + head + 1, :] * share
+            mixed = own_acc[head] * share
+            for slot, other in zip(slots, tops):
+                share = stat_in[slot, heads + head : heads + head + 1, :] * jnp.exp(other - best)
+                total = total + share
+                mixed = mixed + part_in[slot, head].astype(F32) * share
+            att_v[:, head_cols(head)] = (mixed / total).T.astype(BF16)
+
+    @pl.when(me < 2)
+    def _():
+        finish([])
+
+    @pl.when(me == 2)
+    def _():
+        send_part_near.wait_recv()
+        send_stat_near.wait_recv()
+        finish([0])
+
+    @pl.when(me == 3)
+    def _():
+        send_part_last.wait_recv()
+        send_stat_last.wait_recv()
+        send_part_far.wait_recv()
+        send_stat_far.wait_recv()
+        finish([0, 1])
+
+    attention_write = pltpu.make_async_copy(att_v, attention_out, out_sem.at[1])
+    attention_write.start()
+
+    for copy in cache_copies:
+        copy.wait_send()
+
+    @pl.when(me < 3)
+    def _():
+        send_product.wait_send()
+
+    @pl.when(me == 0)
+    def _():
+        send_k.wait_send()
+        send_v.wait_send()
+
+    @pl.when(me == 1)
+    def _():
+        for copy in (send_part_near, send_stat_near, send_part_far, send_stat_far):
+            copy.wait_send()
+
+    @pl.when(me == 2)
+    def _():
+        for copy in (send_q2, send_part_last, send_stat_last):
+            copy.wait_send()
+
+    @pl.when(me == 3)
+    def _():
+        send_q3.wait_send()
+        send_q3_near.wait_send()
+
+    hyena_write.wait()
+    attention_write.wait()
+
+
+def short_form(
+    x_gate, x_key, x_value, conv_state, filter_taps, decay_rates, skip_gain,
+    queries, stretch_keys, stretch_values, cache_keys, cache_values, prefix_len,
+):
+    rows, chans = x_gate.shape
+    groups, taps = filter_taps.shape
+    across = queries.shape[1]
+    heads = across // HD
+    cache_rows = cache_keys.shape[0]
+    any_spec = pl.BlockSpec(memory_space=pltpu.HBM)
+    dma = pltpu.SemaphoreType.DMA
+    vm = pltpu.VMEM
+    return pl.pallas_call(
+        short_kernel,
+        out_shape=(
+            jax.ShapeDtypeStruct((rows, chans), BF16),
+            jax.ShapeDtypeStruct((rows, across), BF16),
+        ),
+        in_specs=[any_spec] * 12 + [pl.BlockSpec(memory_space=pltpu.SMEM)],
+        out_specs=(any_spec, any_spec),
+        scratch_shapes=[
+            vm((rows, chans), BF16),
+            vm((rows, chans), BF16),
+            vm((rows, chans), BF16),
+            vm((rows - 1, chans), BF16),
+            vm((groups, taps), F32),
+            vm((1, groups), F32),
+            vm((1, chans), F32),
+            vm((rows, across), BF16),
+            vm((rows, across), BF16),
+            vm((rows, across), BF16),
+            vm((4, cache_rows, across), BF16),
+            vm((4, cache_rows, across), BF16),
+            vm((rows, across), BF16),
+            vm((rows, across), BF16),
+            vm((2, rows, across), BF16),
+            vm((rows, chans), BF16),
+            vm((rows, chans), BF16),
+            vm((rows, chans), F32),
+            vm((groups, taps), F32),
+            vm((groups // 2, rows, 2 * taps), BF16),
+            vm((groups // 2, rows, 2 * taps), BF16),
+            vm((rows, chans), F32),
+            vm((rows, chans), BF16),
+            vm((heads, HD, rows), F32),
+            vm((2 * heads, rows), F32),
+            vm((2, heads, HD, rows), BF16),
+            vm((2, 2 * heads, rows), F32),
+            vm((2, heads, HD, rows), BF16),
+            vm((2, 2 * heads, rows), F32),
+            vm((rows, across), BF16),
+            dma((12,)),
+            dma((9,)),
+            dma((9,)),
+            dma((2, 3)),
+            dma((2, 4)),
+            dma((2,)),
+        ],
+        compiler_params=pltpu.CompilerParams(
+            collective_id=0, has_side_effects=True, vmem_limit_bytes=48 << 20
+        ),
+    )(
+        x_gate, x_key, x_value, conv_state, filter_taps,
+        decay_rates.reshape(1, groups), skip_gain.reshape(1, chans),
+        queries, stretch_keys, stretch_values, cache_keys, cache_values, prefix_len,
+    )
+
+
+def on_device(*arrays):
+    rows, taps = arrays[0].shape[0], arrays[4].shape[1]
+    if lax.axis_size("seq") == 4 and rows == taps == 128:
+        return short_form(*arrays)
+    return general_form(*arrays)
+
+
 def solution(mesh):
     placed = (
         P(("parts", "seq"), "tp"),

time: 128 us -> 32.6 us (0.25)
  the two profiles are of different devices: /device:TPU:0 before, /device:TPU:16 now
where the time goes in v1:
time: 32.6 us; the launch traced here: 32.1 us
  Pallas kernels  20.1 us (62%)
  local copies, waits for them, and re-layouts  10.7 us (33%)
  between operations  1.33 us (4%)
    pallas_call x1, Pallas kernels, short_form(): pl.pallas_call(short_kernel, out_shape=(jax.ShapeDtypeStruct((rows, chans...  20.1 us
    unnamed x26, local copies, waits for them, and re-layouts  10.7 us

profile of v1, /device:TPU:16, one launch (start us, length us, event | category | flops | bytes accessed | tf_op | source)
XLA Modules:
  0.0 32.1 jit_solution(14128381180017955516)
XLA Ops:
  0.6 0.0 copy-start.10
  1.3 0.0 copy-start.11
  1.3 0.0 copy-done.10
  1.3 0.6 %copy-done.11 = f32[64]{0:T(128)S(1)} copy-done((f32[64]{0:T(128)S(1)}, f32[64]{0:T(128)}, u32[]{:S(2)}) %copy-start.11) | copy-done | bytes 280
  2.0 0.0 copy-start
  2.0 0.9 %copy-done = bf16[128,1024]{1,0:T(8,128)(2,1)S(1)} copy-done((bf16[128,1024]{1,0:T(8,128)(2,1)S(1)}, bf16[128,1024]{1,0:T(8,128)(2,1)}, u32[]{:S(2)}) %copy-start) | copy-done | bytes 262168
  2.9 0.0 copy-start.1
  2.9 0.9 %copy-done.1 = bf16[128,1024]{1,0:T(8,128)(2,1)S(1)} copy-done((bf16[128,1024]{1,0:T(8,128)(2,1)S(1)}, bf16[128,1024]{1,0:T(8,128)(2,1)}, u32[]{:S(2)}) %copy-start.1) | copy-done | bytes 262168
  3.9 0.0 copy-start.2
  3.9 0.9 %copy-done.2 = bf16[128,1024]{1,0:T(8,128)(2,1)S(1)} copy-done((bf16[128,1024]{1,0:T(8,128)(2,1)S(1)}, bf16[128,1024]{1,0:T(8,128)(2,1)}, u32[]{:S(2)}) %copy-start.2) | copy-done | bytes 262168
  4.8 0.0 copy-start.3
  4.8 0.9 %copy-done.3 = bf16[127,1024]{1,0:T(8,128)(2,1)S(1)} copy-done((bf16[127,1024]{1,0:T(8,128)(2,1)S(1)}, bf16[127,1024]{1,0:T(8,128)(2,1)}, u32[]{:S(2)}) %copy-start.3) | copy-done | bytes 260120
  5.8 0.0 copy-start.4
  5.8 0.9 %copy-done.4 = bf16[128,512]{1,0:T(8,128)(2,1)S(1)} copy-done((bf16[128,512]{1,0:T(8,128)(2,1)S(1)}, bf16[128,512]{1,0:T(8,128)(2,1)}, u32[]{:S(2)}) %copy-start.4) | copy-done | bytes 131096
  6.7 0.0 copy-start.5
  6.7 0.9 %copy-done.5 = bf16[128,512]{1,0:T(8,128)(2,1)S(1)} copy-done((bf16[128,512]{1,0:T(8,128)(2,1)S(1)}, bf16[128,512]{1,0:T(8,128)(2,1)}, u32[]{:S(2)}) %copy-start.5) | copy-done | bytes 131096
  7.6 0.0 copy-start.6
  7.6 0.9 %copy-done.6 = bf16[128,512]{1,0:T(8,128)(2,1)S(1)} copy-done((bf16[128,512]{1,0:T(8,128)(2,1)S(1)}, bf16[128,512]{1,0:T(8,128)(2,1)}, u32[]{:S(2)}) %copy-start.6) | copy-done | bytes 131096
  8.5 0.0 copy-start.7
  8.5 0.8 %copy-done.7 = f32[64,128]{1,0:T(8,128)S(1)} copy-done((f32[64,128]{1,0:T(8,128)S(1)}, f32[64,128]{1,0:T(8,128)}, u32[]{:S(2)}) %copy-start.7) | copy-done | bytes 32792
  9.2 0.0 copy-start.8
  9.2 0.7 %copy-done.8 = bf16[8,512]{1,0:T(8,128)(2,1)S(1)} copy-done((bf16[8,512]{1,0:T(8,128)(2,1)S(1)}, bf16[8,512]{1,0:T(8,128)(2,1)}, u32[]{:S(2)}) %copy-start.8) | copy-done | bytes 8216
  9.9 0.0 copy-start.9
  9.9 0.7 %copy-done.9 = bf16[8,512]{1,0:T(8,128)(2,1)S(1)} copy-done((bf16[8,512]{1,0:T(8,128)(2,1)S(1)}, bf16[8,512]{1,0:T(8,128)(2,1)}, u32[]{:S(2)}) %copy-start.9) | copy-done | bytes 8216
  10.6 20.1 %shard_map.140 = (bf16[128,1024]{1,0:T(8,128)(2,1)S(1)}, bf16[128,512]{1,0:T(8,128)(2,1)S(1)}) custom-call(bf16[128,1024]{1,0:T(8,128)(2,1)S(1)} %copy-done, bf16[128,1024]{1,0:T(8,128)(2,1)S(1)} %copy-done.1, bf16[128,1024]{1,0:T(8,128)(2,1)S(1)} %copy-done.2, bf16[127,1024]{1,0:T(8,128)(2,1)S(1)} %copy-done.3, f32[64,128]{1,0:T(8,128)S(1)} %copy-done.7, ...), custom_call_target="tpu_custom_call" | custom-call | tf_op jit(solution)/shard_map/pallas_call | solution.py:556
  30.7 0.7 %copy.18 = bf16[128,1024]{1,0:T(8,128)(2,1)} copy(bf16[128,1024]{1,0:T(8,128)(2,1)S(1)} %get-tuple-element.4) | data formatting | bytes 524288
  31.5 0.7 %copy.19 = bf16[128,512]{1,0:T(8,128)(2,1)} copy(bf16[128,512]{1,0:T(8,128)(2,1)S(1)} %get-tuple-element.5) | data formatting | bytes 262144
Async XLA Ops:
  0.6 0.7 %copy-start.10 = (f32[1024]{0:T(1024)S(1)}, f32[1024]{0:T(1024)}, u32[]{:S(2)}) copy-start(f32[1024]{0:T(1024)} %param.19) | copy-start | bytes 12292
  1.3 0.7 %copy-start.11 = (f32[64]{0:T(128)S(1)}, f32[64]{0:T(128)}, u32[]{:S(2)}) copy-start(f32[64]{0:T(128)} %param.18) | copy-start | bytes 772
  2.0 0.9 %copy-start = (bf16[128,1024]{1,0:T(8,128)(2,1)S(1)}, bf16[128,1024]{1,0:T(8,128)(2,1)}, u32[]{:S(2)}) copy-start(bf16[128,1024]{1,0:T(8,128)(2,1)} %x_gate.1) | copy-start | bytes 786436
  2.9 0.9 %copy-start.1 = (bf16[128,1024]{1,0:T(8,128)(2,1)S(1)}, bf16[128,1024]{1,0:T(8,128)(2,1)}, u32[]{:S(2)}) copy-start(bf16[128,1024]{1,0:T(8,128)(2,1)} %x_key.1) | copy-start | bytes 786436
  3.9 0.9 %copy-start.2 = (bf16[128,1024]{1,0:T(8,128)(2,1)S(1)}, bf16[128,1024]{1,0:T(8,128)(2,1)}, u32[]{:S(2)}) copy-start(bf16[128,1024]{1,0:T(8,128)(2,1)} %x_value.1) | copy-start | bytes 786436
  4.8 0.9 %copy-start.3 = (bf16[127,1024]{1,0:T(8,128)(2,1)S(1)}, bf16[127,1024]{1,0:T(8,128)(2,1)}, u32[]{:S(2)}) copy-start(bf16[127,1024]{1,0:T(8,128)(2,1)} %conv_state.1) | copy-start | bytes 780292
  5.8 0.9 %copy-start.4 = (bf16[128,512]{1,0:T(8,128)(2,1)S(1)}, bf16[128,512]{1,0:T(8,128)(2,1)}, u32[]{:S(2)}) copy-start(bf16[128,512]{1,0:T(8,128)(2,1)} %queries.1) | copy-start | bytes 393220
  6.7 0.9 %copy-start.5 = (bf16[128,512]{1,0:T(8,128)(2,1)S(1)}, bf16[128,512]{1,0:T(8,128)(2,1)}, u32[]{:S(2)}) copy-start(bf16[128,512]{1,0:T(8,128)(2,1)} %stretch_keys.1) | copy-start | bytes 393220
  7.6 0.9 %copy-start.6 = (bf16[128,512]{1,0:T(8,128)(2,1)S(1)}, bf16[128,512]{1,0:T(8,128)(2,1)}, u32[]{:S(2)}) copy-start(bf16[128,512]{1,0:T(8,128)(2,1)} %stretch_values.1) | copy-start | bytes 393220
  8.5 0.8 %copy-start.7 = (f32[64,128]{1,0:T(8,128)S(1)}, f32[64,128]{1,0:T(8,128)}, u32[]{:S(2)}) copy-start(f32[64,128]{1,0:T(8,128)} %filter_taps.1) | copy-start | bytes 98308
  9.2 0.7 %copy-start.8 = (bf16[8,512]{1,0:T(8,128)(2,1)S(1)}, bf16[8,512]{1,0:T(8,128)(2,1)}, u32[]{:S(2)}) copy-start(bf16[8,512]{1,0:T(8,128)(2,1)} %cache_keys.1) | copy-start | bytes 24580
  9.9 0.7 %copy-start.9 = (bf16[8,512]{1,0:T(8,128)(2,1)S(1)}, bf16[8,512]{1,0:T(8,128)(2,1)}, u32[]{:S(2)}) copy-start(bf16[8,512]{1,0:T(8,128)(2,1)} %cache_values.1) | copy-start | bytes 24580

commit v2 on v1

--- a/solution.py
+++ b/solution.py
@@ -600,7 +600,7 @@
             dma((2,)),
         ],
         compiler_params=pltpu.CompilerParams(
-            collective_id=0, has_side_effects=True, vmem_limit_bytes=48 << 20
+            collective_id=0, has_side_effects=True, vmem_limit_bytes=56 << 20
         ),
     )(
         x_gate, x_key, x_value, conv_state, filter_taps,

time: 32.6 us -> 24 us (0.74)
  local copies, waits for them, and re-layouts: 10.7 us -> 2.36 us
    unnamed x26 -> x4, local copies, waits for them, and re-layouts: 10.7 us -> 2.36 us
where the time goes in v2:
time: 24 us; the launch traced here: 23.8 us
  Pallas kernels  20.2 us (84%)
  local copies, waits for them, and re-layouts  2.36 us (10%)
  between operations  1.3 us (5%)
    pallas_call x1, Pallas kernels, short_form(): pl.pallas_call(short_kernel, out_shape=(jax.ShapeDtypeStruct((rows, chans...  20.2 us
    unnamed x4, local copies, waits for them, and re-layouts  2.36 us

profile of v2, /device:TPU:16, one launch (start us, length us, event | category | flops | bytes accessed | tf_op | source)
XLA Modules:
  0.0 23.8 jit_solution(15089288982965716574)
XLA Ops:
  1.3 20.2 %shard_map.140 = (bf16[128,1024]{1,0:T(8,128)(2,1)}, bf16[128,512]{1,0:T(8,128)(2,1)}) custom-call(bf16[128,1024]{1,0:T(8,128)(2,1)} %x_gate.1, bf16[128,1024]{1,0:T(8,128)(2,1)} %x_key.1, bf16[128,1024]{1,0:T(8,128)(2,1)} %x_value.1, bf16[127,1024]{1,0:T(8,128)(2,1)} %conv_state.1, f32[64,128]{1,0:T(8,128)} %filter_taps.1, f32[1,64]{1,0:T(1,128)} %bitcast.3, ...), custom_call_target="tpu_custom_call" | custom-call | tf_op jit(solution)/shard_map/pallas_call | solution.py:556
  21.4 0.0 copy-start
  21.5 1.7 %copy.18 = bf16[128,1024]{1,0:T(8,128)(2,1)} copy(bf16[128,1024]{1,0:T(8,128)(2,1)} %get-tuple-element.4) | data formatting | bytes 524288
  23.2 0.0 copy-done
  23.2 0.7 %copy.19 = bf16[128,512]{1,0:T(8,128)(2,1)} copy(bf16[128,512]{1,0:T(8,128)(2,1)S(1)} %copy-done) | data formatting | bytes 262144
Async XLA Ops:
  21.4 1.7 %copy-start = (bf16[128,512]{1,0:T(8,128)(2,1)S(1)}, bf16[128,512]{1,0:T(8,128)(2,1)}, u32[]{:S(2)}) copy-start(bf16[128,512]{1,0:T(8,128)(2,1)} %get-tuple-element.5) | copy-start | bytes 393220

commit v3 on v2

--- a/solution.py
+++ b/solution.py
@@ -194,12 +194,12 @@
 def short_kernel(
     x_gate, x_key, x_value, conv_state, filter_taps, decay_rates, skip_gain,
     queries, stretch_keys, stretch_values, cache_keys, cache_values, prefix_len,
-    hyena_out, attention_out,
+    out_v, att_v,
     gate_v, key_v, value_v, state_v, taps_v, decay_v, skip_v, q_v, k_v, v_v,
     cache_k, cache_v, k_in, v_in, q_in, product_v, earlier_v, shifted_v,
-    reversed_v, lower_v, upper_v, local_v, out_v,
-    own_acc, own_stat, part_out, stat_out, part_in, stat_in, att_v,
-    load_sem, send_sem, recv_sem, cache_send, cache_recv, out_sem,
+    reversed_v, lower_v, upper_v, local_v,
+    own_acc, own_stat, part_out, stat_out, part_in, stat_in,
+    load_sem, send_sem, recv_sem, part_send, part_recv, cache_send, cache_recv,
 ):
     me = lax.axis_index("seq")
     rows, chans = gate_v.shape
@@ -240,15 +240,23 @@
     send_q2 = remote(queries, q_in.at[0], send_sem.at[2], recv_sem.at[2], 1)
     send_q3 = remote(queries, q_in.at[1], send_sem.at[3], recv_sem.at[3], 1)
     send_q3_near = remote(queries, q_in.at[1], send_sem.at[2], recv_sem.at[3], 2)
-    send_product = remote(
-        product_v, earlier_v, send_sem.at[4], recv_sem.at[4], lax.rem(me + 1, 4)
-    )
-    send_part_near = remote(part_out.at[0], part_in.at[0], send_sem.at[5], recv_sem.at[5], 2)
-    send_stat_near = remote(stat_out.at[0], stat_in.at[0], send_sem.at[6], recv_sem.at[6], 2)
-    send_part_far = remote(part_out.at[1], part_in.at[0], send_sem.at[7], recv_sem.at[5], 3)
-    send_stat_far = remote(stat_out.at[1], stat_in.at[0], send_sem.at[8], recv_sem.at[6], 3)
-    send_part_last = remote(part_out.at[1], part_in.at[1], send_sem.at[5], recv_sem.at[7], 3)
-    send_stat_last = remote(stat_out.at[1], stat_in.at[1], send_sem.at[6], recv_sem.at[8], 3)
+    send_product = [
+        remote(
+            product_v.at[:, pl.ds(half * chans // 2, chans // 2)],
+            earlier_v.at[:, pl.ds(half * chans // 2, chans // 2)],
+            send_sem.at[4 + half], recv_sem.at[4 + half], lax.rem(me + 1, 4),
+        )
+        for half in range(2)
+    ]
+
+    def send_part(slot, landing, head, target):
+        return [
+            remote(
+                src.at[slot, head], dst.at[landing, head],
+                part_send.at[which, slot, head], part_recv.at[which, landing, head], target,
+            )
+            for which, (src, dst) in enumerate([(part_out, part_in), (stat_out, stat_in)])
+        ]
 
     @pl.when(me == 0)
     def _():
@@ -280,9 +288,10 @@
     loads["value"].wait()
     product_v[...] = (key_v[...].astype(F32) * value_v[...].astype(F32)).astype(BF16)
 
-    @pl.when(me < 3)
-    def _():
-        send_product.start()
+    @pl.when((me > 0) & (me < 3))
+    def _():
+        for copy in send_product:
+            copy.start()
 
     loads["taps"].wait()
     loads["decay"].wait()
@@ -335,6 +344,13 @@
         cols = slice(tile * 128, (tile + 1) * 128)
         block = product_v[:, cols]
         local_v[:, cols] = filtered(lower_v, block, tile) + skip_v[:, cols] * block.astype(F32)
+
+    @pl.when(me == 0)
+    def _():
+        send_k.wait_send()
+        send_v.wait_send()
+        for copy in send_product:
+            copy.start()
 
     loads["q"].wait()
     loads["k"].wait()
@@ -405,8 +421,8 @@
         own_acc[head] = result[2]
 
     def give(slot, head, result):
-        stat_out[slot, head : head + 1, :] = result[0]
-        stat_out[slot, heads + head : heads + head + 1, :] = result[1]
+        stat_out[slot, head, 0:1, :] = result[0]
+        stat_out[slot, head, 1:2, :] = result[1]
         part_out[slot, head] = (result[2] / result[1]).astype(BF16)
 
     @pl.when(me != 1)
@@ -425,16 +441,13 @@
                 (k_v[:, cols], v_v[:, cols], None),
             ]
 
-        for slot, arrival, part, stat in (
-            (1, send_q3, send_part_far, send_stat_far),
-            (0, send_q2, send_part_near, send_stat_near),
-        ):
+        for slot, arrival, target in ((1, send_q3, 3), (0, send_q2, 2)):
             arrival.wait_recv()
             for head in range(heads):
                 cols = head_cols(head)
                 give(slot, head, attend(q_in[slot, :, cols], shared_blocks(cols)))
-            part.start()
-            stat.start()
+                for copy in send_part(slot, 0, head, target):
+                    copy.start()
         for head in range(heads):
             cols = head_cols(head)
             keep(
@@ -450,8 +463,8 @@
         for head in range(heads):
             cols = head_cols(head)
             give(1, head, attend(q_in[1, :, cols], [(k_v[:, cols], v_v[:, cols], None)]))
-        send_part_last.start()
-        send_stat_last.start()
+            for copy in send_part(1, 1, head, 3):
+                copy.start()
 
     loads["state"].wait()
 
@@ -461,22 +474,26 @@
         shifted_v[pl.ds(1, rows - 1), :] = state_v[...].astype(F32)
         earlier_v[...] = shifted_v[...].astype(BF16)
 
-    @pl.when(me > 0)
-    def _():
-        send_product.wait_recv()
-
     loads["gate"].wait()
-    for tile in range(chans // 128):
+    tiles = chans // 128
+    for tile in range(tiles):
+        if tile % (tiles // 2) == 0:
+
+            @pl.when(me > 0)
+            def _():
+                send_product[tile // (tiles // 2)].wait_recv()
+
         cols = slice(tile * 128, (tile + 1) * 128)
         whole = local_v[:, cols] + filtered(upper_v, earlier_v[:, cols], tile)
         out_v[:, cols] = (gate_v[:, cols].astype(F32) * whole).astype(BF16)
-    hyena_write = pltpu.make_async_copy(out_v, hyena_out, out_sem.at[0])
-    hyena_write.start()
 
     def finish(slots):
         for head in range(heads):
+            for slot in slots:
+                for copy in send_part(1, slot, head, 1):
+                    copy.wait_recv()
             top = own_stat[head : head + 1, :]
-            tops = [stat_in[slot, head : head + 1, :] for slot in slots]
+            tops = [stat_in[slot, head, 0:1, :] for slot in slots]
             best = top
             for other in tops:
                 best = jnp.maximum(best, other)
@@ -484,7 +501,7 @@
             total = own_stat[heads + head : heads + head + 1, :] * share
             mixed = own_acc[head] * share
             for slot, other in zip(slots, tops):
-                share = stat_in[slot, heads + head : heads + head + 1, :] * jnp.exp(other - best)
+                share = stat_in[slot, head, 1:2, :] * jnp.exp(other - best)
                 total = total + share
                 mixed = mixed + part_in[slot, head].astype(F32) * share
             att_v[:, head_cols(head)] = (mixed / total).T.astype(BF16)
@@ -495,50 +512,37 @@
 
     @pl.when(me == 2)
     def _():
-        send_part_near.wait_recv()
-        send_stat_near.wait_recv()
         finish([0])
 
     @pl.when(me == 3)
     def _():
-        send_part_last.wait_recv()
-        send_stat_last.wait_recv()
-        send_part_far.wait_recv()
-        send_stat_far.wait_recv()
-        finish([0, 1])
-
-    attention_write = pltpu.make_async_copy(att_v, attention_out, out_sem.at[1])
-    attention_write.start()
+        finish([1, 0])
 
     for copy in cache_copies:
         copy.wait_send()
 
     @pl.when(me < 3)
     def _():
-        send_product.wait_send()
-
-    @pl.when(me == 0)
-    def _():
-        send_k.wait_send()
-        send_v.wait_send()
+        for copy in send_product:
+            copy.wait_send()
 
     @pl.when(me == 1)
     def _():
-        for copy in (send_part_near, send_stat_near, send_part_far, send_stat_far):
-            copy.wait_send()
+        for head in range(heads):
+            for copy in send_part(1, 0, head, 3) + send_part(0, 0, head, 2):
+                copy.wait_send()
 
     @pl.when(me == 2)
     def _():
-        for copy in (send_q2, send_part_last, send_stat_last):
-            copy.wait_send()
+        send_q2.wait_send()
+        for head in range(heads):
+            for copy in send_part(1, 1, head, 3):
+                copy.wait_send()
 
     @pl.when(me == 3)
     def _():
         send_q3.wait_send()
         send_q3_near.wait_send()
-
-    hyena_write.wait()
-    attention_write.wait()
 
 
 def short_form(
@@ -560,7 +564,7 @@
             jax.ShapeDtypeStruct((rows, across), BF16),
         ),
         in_specs=[any_spec] * 12 + [pl.BlockSpec(memory_space=pltpu.SMEM)],
-        out_specs=(any_spec, any_spec),
+        out_specs=(pl.BlockSpec(memory_space=pltpu.VMEM),) * 2,
         scratch_shapes=[
             vm((rows, chans), BF16),
             vm((rows, chans), BF16),
@@ -584,28 +588,33 @@
             vm((groups // 2, rows, 2 * taps), BF16),
             vm((groups // 2, rows, 2 * taps), BF16),
             vm((rows, chans), F32),
-            vm((rows, chans), BF16),
             vm((heads, HD, rows), F32),
             vm((2 * heads, rows), F32),
             vm((2, heads, HD, rows), BF16),
-            vm((2, 2 * heads, rows), F32),
+            vm((2, heads, 2, rows), F32),
             vm((2, heads, HD, rows), BF16),
-            vm((2, 2 * heads, rows), F32),
-            vm((rows, across), BF16),
+            vm((2, heads, 2, rows), F32),
             dma((12,)),
-            dma((9,)),
-            dma((9,)),
+            dma((6,)),
+            dma((6,)),
+            dma((2, 2, heads)),
+            dma((2, 2, heads)),
             dma((2, 3)),
             dma((2, 4)),
-            dma((2,)),
         ],
         compiler_params=pltpu.CompilerParams(
-            collective_id=0, has_side_effects=True, vmem_limit_bytes=56 << 20
+            collective_id=0, has_side_effects=True, vmem_limit_bytes=40 << 20
         ),
     )(
-        x_gate, x_key, x_value, conv_state, filter_taps,
-        decay_rates.reshape(1, groups), skip_gain.reshape(1, chans),
-        queries, stretch_keys, stretch_values, cache_keys, cache_values, prefix_len,
+        *(
+            pltpu.with_memory_space_constraint(array, pltpu.HBM)
+            for array in (
+                x_gate, x_key, x_value, conv_state, filter_taps,
+                decay_rates.reshape(1, groups), skip_gain.reshape(1, chans),
+                queries, stretch_keys, stretch_values, cache_keys, cache_values,
+            )
+        ),
+        prefix_len,
     )
 
 

time: 24 us -> 21.9 us (0.912)
  Pallas kernels: 20.2 us -> 19.1 us
  local copies, waits for them, and re-layouts: 2.36 us -> 1.36 us
    pallas_call x1, Pallas kernels: 20.2 us -> 19.1 us  [short_form(): pl.pallas_call(short_kernel, out_shape=(jax.ShapeDtypeStruct((rows, chans...]
    unnamed x4 -> x2, local copies, waits for them, and re-layouts: 2.36 us -> 1.36 us
where the time goes in v3:
time: 21.9 us; the launch traced here: 21.7 us
  Pallas kernels  19.1 us (87%)
  local copies, waits for them, and re-layouts  1.36 us (6%)
  between operations  1.29 us (6%)
    pallas_call x1, Pallas kernels, short_form(): pl.pallas_call(short_kernel, out_shape=(jax.ShapeDtypeStruct((rows, chans...  19.1 us
    unnamed x2, local copies, waits for them, and re-layouts  1.36 us

profile of v3, /device:TPU:16, one launch (start us, length us, event | category | flops | bytes accessed | tf_op | source)
XLA Modules:
  0.0 21.7 jit_solution(13103664234430581302)
XLA Ops:
  1.3 19.1 %shard_map.140 = (bf16[128,1024]{1,0:T(8,128)(2,1)S(1)}, bf16[128,512]{1,0:T(8,128)(2,1)S(1)}) custom-call(bf16[128,1024]{1,0:T(8,128)(2,1)} %x_gate.1, bf16[128,1024]{1,0:T(8,128)(2,1)} %x_key.1, bf16[128,1024]{1,0:T(8,128)(2,1)} %x_value.1, bf16[127,1024]{1,0:T(8,128)(2,1)} %conv_state.1, f32[64,128]{1,0:T(8,128)} %filter_taps.1, f32[1,64]{1,0:T(1,128)} %bitcast.3, ...), custom_call_target="tpu_custom_call" | custom-call | tf_op jit(solution)/shard_map/pallas_call | solution.py:560
  20.4 0.7 %copy.18 = bf16[128,1024]{1,0:T(8,128)(2,1)} copy(bf16[128,1024]{1,0:T(8,128)(2,1)S(1)} %get-tuple-element.4) | data formatting | bytes 524288
  21.1 0.7 %copy.19 = bf16[128,512]{1,0:T(8,128)(2,1)} copy(bf16[128,512]{1,0:T(8,128)(2,1)S(1)} %get-tuple-element.5) | data formatting | bytes 262144

commit v4 on v3

--- a/solution.py
+++ b/solution.py
@@ -545,6 +545,17 @@
         send_q3_near.wait_send()
 
 
+def store_kernel(hyena_in, attention_in, hyena_out, attention_out, sem):
+    copies = [
+        pltpu.make_async_copy(hyena_in, hyena_out, sem.at[0]),
+        pltpu.make_async_copy(attention_in, attention_out, sem.at[1]),
+    ]
+    for copy in copies:
+        copy.start()
+    for copy in copies:
+        copy.wait()
+
+
 def short_form(
     x_gate, x_key, x_value, conv_state, filter_taps, decay_rates, skip_gain,
     queries, stretch_keys, stretch_values, cache_keys, cache_values, prefix_len,
@@ -557,11 +568,11 @@
     any_spec = pl.BlockSpec(memory_space=pltpu.HBM)
     dma = pltpu.SemaphoreType.DMA
     vm = pltpu.VMEM
-    return pl.pallas_call(
+    held = pl.pallas_call(
         short_kernel,
         out_shape=(
-            jax.ShapeDtypeStruct((rows, chans), BF16),
-            jax.ShapeDtypeStruct((rows, across), BF16),
+            pltpu.VMEM((rows, chans), BF16),
+            pltpu.VMEM((rows, across), BF16),
         ),
         in_specs=[any_spec] * 12 + [pl.BlockSpec(memory_space=pltpu.SMEM)],
         out_specs=(pl.BlockSpec(memory_space=pltpu.VMEM),) * 2,
@@ -616,6 +627,17 @@
         ),
         prefix_len,
     )
+    return pl.pallas_call(
+        store_kernel,
+        out_shape=(
+            jax.ShapeDtypeStruct((rows, chans), BF16),
+            jax.ShapeDtypeStruct((rows, across), BF16),
+        ),
+        in_specs=[pl.BlockSpec(memory_space=pltpu.VMEM)] * 2,
+        out_specs=(any_spec, any_spec),
+        scratch_shapes=[dma((2,))],
+        compiler_params=pltpu.CompilerParams(vmem_limit_bytes=40 << 20),
+    )(*(pltpu.with_memory_space_constraint(array, pltpu.VMEM) for array in held))
 
 
 def on_device(*arrays):

time: 21.9 us -> 21.3 us (0.973)
  local copies, waits for them, and re-layouts: 1.36 us -> 0 us
  Pallas kernels: 19.1 us -> 19.8 us
    unnamed x2 -> x0, local copies, waits for them, and re-layouts: 1.36 us -> none
    pallas_call x1 -> x2, Pallas kernels: 19.1 us -> 19.8 us  [the longest x1 19.1 us: short_form(): pl.pallas_call(short_kernel, out_shape=(pltpu.VMEM((rows, chans), BF16),...]
where the time goes in v4:
time: 21.3 us; the launch traced here: 21.1 us
  Pallas kernels  19.8 us (93%)
  between operations  1.29 us (6%)
    pallas_call x1, Pallas kernels, short_form(): pl.pallas_call(short_kernel, out_shape=(pltpu.VMEM((rows, chans), BF16),...  19.1 us
    pallas_call x1, Pallas kernels, short_form(): pl.pallas_call(store_kernel, out_shape=(jax.ShapeDtypeStruct((rows, chans...  0.76 us

profile of v4, /device:TPU:16, one launch (start us, length us, event | category | flops | bytes accessed | tf_op | source)
XLA Modules:
  0.0 21.1 jit_solution(8950326732605671255)
XLA Ops:
  1.3 19.1 %shard_map.140 = (bf16[128,1024]{1,0:T(8,128)(2,1)S(1)}, bf16[128,512]{1,0:T(8,128)(2,1)S(1)}) custom-call(bf16[128,1024]{1,0:T(8,128)(2,1)} %x_gate.1, bf16[128,1024]{1,0:T(8,128)(2,1)} %x_key.1, bf16[128,1024]{1,0:T(8,128)(2,1)} %x_value.1, bf16[127,1024]{1,0:T(8,128)(2,1)} %conv_state.1, f32[64,128]{1,0:T(8,128)} %filter_taps.1, f32[1,64]{1,0:T(1,128)} %bitcast.3, ...), custom_call_target="tpu_custom_call" | custom-call | tf_op jit(solution)/shard_map/pallas_call | solution.py:571
  20.4 0.8 %shard_map.141 = (bf16[128,1024]{1,0:T(8,128)(2,1)}, bf16[128,512]{1,0:T(8,128)(2,1)}) custom-call(bf16[128,1024]{1,0:T(8,128)(2,1)S(1)} %get-tuple-element.4.hyena_in, bf16[128,512]{1,0:T(8,128)(2,1)S(1)} %get-tuple-element.5.attention_in), custom_call_target="tpu_custom_call" | custom-call | tf_op jit(solution)/shard_map/pallas_call | solution.py:630

commit v5 on v4

--- a/solution.py
+++ b/solution.py
@@ -199,7 +199,7 @@
     cache_k, cache_v, k_in, v_in, q_in, product_v, earlier_v, shifted_v,
     reversed_v, lower_v, upper_v, local_v,
     own_acc, own_stat, part_out, stat_out, part_in, stat_in,
-    load_sem, send_sem, recv_sem, part_send, part_recv, cache_send, cache_recv,
+    load_sem, send_sem, recv_sem, part_send, part_recv, cache_send, cache_recv, ready_sem,
 ):
     me = lax.axis_index("seq")
     rows, chans = gate_v.shape
@@ -230,10 +230,25 @@
 
     barrier = pltpu.get_barrier_semaphore()
     for step in range(1, 4):
-        pl.semaphore_signal(
-            barrier, inc=1, device_id={"seq": lax.rem(me + step, 4)}, device_id_type=MESH
-        )
-    pl.semaphore_wait(barrier, 3)
+        target = lax.rem(me + step, 4)
+
+        @pl.when((target > 0) | (me == 1))
+        def _():
+            pl.semaphore_signal(
+                barrier, inc=1, device_id={"seq": target}, device_id_type=MESH
+            )
+
+    @pl.when(me == 0)
+    def _():
+        pl.semaphore_wait(barrier, 1)
+
+    @pl.when(me > 0)
+    def _():
+        pl.semaphore_wait(barrier, 3)
+
+    @pl.when(me > 1)
+    def _():
+        pl.semaphore_signal(ready_sem, inc=1, device_id={"seq": 0}, device_id_type=MESH)
 
     send_k = remote(stretch_keys, k_in, send_sem.at[0], recv_sem.at[0], 1)
     send_v = remote(stretch_values, v_in, send_sem.at[1], recv_sem.at[1], 1)
@@ -272,6 +287,19 @@
         send_q3.start()
         send_q3_near.start()
 
+    loads["key"].wait()
+    loads["value"].wait()
+    product_v[...] = (key_v[...].astype(F32) * value_v[...].astype(F32)).astype(BF16)
+
+    @pl.when((me > 0) & (me < 3))
+    def _():
+        for copy in send_product:
+            copy.start()
+
+    @pl.when(me == 0)
+    def _():
+        pl.semaphore_wait(ready_sem, 2)
+
     cache_copies = []
     for step in range(1, 4):
         target = lax.rem(me + step, 4)
@@ -283,15 +311,6 @@
             )
             copy.start()
             cache_copies.append(copy)
-
-    loads["key"].wait()
-    loads["value"].wait()
-    product_v[...] = (key_v[...].astype(F32) * value_v[...].astype(F32)).astype(BF16)
-
-    @pl.when((me > 0) & (me < 3))
-    def _():
-        for copy in send_product:
-            copy.start()
 
     loads["taps"].wait()
     loads["decay"].wait()
@@ -441,7 +460,7 @@
                 (k_v[:, cols], v_v[:, cols], None),
             ]
 
-        for slot, arrival, target in ((1, send_q3, 3), (0, send_q2, 2)):
+        for slot, arrival, target in ((0, send_q2, 2), (1, send_q3, 3)):
             arrival.wait_recv()
             for head in range(heads):
                 cols = head_cols(head)
@@ -612,6 +631,7 @@
             dma((2, 2, heads)),
             dma((2, 3)),
             dma((2, 4)),
+            pltpu.SemaphoreType.REGULAR,
         ],
         compiler_params=pltpu.CompilerParams(
             collective_id=0, has_side_effects=True, vmem_limit_bytes=40 << 20

time: 21.3 us -> 21.1 us (level)
  the two profiles are of different devices: /device:TPU:16 before, /device:TPU:28 now
where the time goes in v5:
time: 21.1 us; the launch traced here: 21 us
  Pallas kernels  19.7 us (93%)
  between operations  1.29 us (6%)
    pallas_call x1, Pallas kernels, short_form(): pl.pallas_call(short_kernel, out_shape=(pltpu.VMEM((rows, chans), BF16),...  18.9 us
    pallas_call x1, Pallas kernels, short_form(): pl.pallas_call(store_kernel, out_shape=(jax.ShapeDtypeStruct((rows, chans...  0.76 us

profile of v5, /device:TPU:28, one launch (start us, length us, event | category | flops | bytes accessed | tf_op | source)
XLA Modules:
  0.0 21.0 jit_solution(7523142115636363654)
XLA Ops:
  1.3 18.9 %shard_map.140 = (bf16[128,1024]{1,0:T(8,128)(2,1)S(1)}, bf16[128,512]{1,0:T(8,128)(2,1)S(1)}) custom-call(bf16[128,1024]{1,0:T(8,128)(2,1)} %x_gate.1, bf16[128,1024]{1,0:T(8,128)(2,1)} %x_key.1, bf16[128,1024]{1,0:T(8,128)(2,1)} %x_value.1, bf16[127,1024]{1,0:T(8,128)(2,1)} %conv_state.1, f32[64,128]{1,0:T(8,128)} %filter_taps.1, f32[1,64]{1,0:T(1,128)} %bitcast.3, ...), custom_call_target="tpu_custom_call" | custom-call | tf_op jit(solution)/shard_map/pallas_call | solution.py:590
  20.2 0.8 %shard_map.141 = (bf16[128,1024]{1,0:T(8,128)(2,1)}, bf16[128,512]{1,0:T(8,128)(2,1)}) custom-call(bf16[128,1024]{1,0:T(8,128)(2,1)S(1)} %get-tuple-element.4.hyena_in, bf16[128,512]{1,0:T(8,128)(2,1)S(1)} %get-tuple-element.5.attention_in), custom_call_target="tpu_custom_call" | custom-call | tf_op jit(solution)/shard_map/pallas_call | solution.py:650
